TPU v7x, 128 devices: a whole 4x4x4 slice. The times are simulated.
128 devices in a mesh: grp: 8 (over z, core), ep: 16 (over x, y).
Axes of the slice: x: 4, y: 4, z: 4, core: 2. Of those that a mesh axis runs over, the one named last changes fastest.
Arguments:
- hidden_in: bfloat16 [16384, 2048], P(('grp', 'ep')), may hold values from -24 to 24
- prompt_lengths: int32 [8, 5], P('grp'), may hold values from 1 to 1024, 2048 in all within a row
- routes: int32 [16384, 6], P(('grp', 'ep')), may hold values from 0 to 63, all different within a row; in each aligned block of 128 rows (0 to 127, 128 to 255, ...) at most 16 rows name the same one
- route_weights: float32 [16384, 6], P(('grp', 'ep')), may hold values from 0.05 to 0.4
- w_query: bfloat16 [2048, 2048], P(None, 'ep'), may hold values from -3 to 3
- w_key: bfloat16 [2048, 2048], P(None, 'ep'), may hold values from -3 to 3
- w_value: bfloat16 [2048, 2048], P(None, 'ep'), may hold values from -0.125 to 0.125
- w_out: bfloat16 [2048, 2048], replicated, may hold values from -0.125 to 0.125
- shared_gate: bfloat16 [2048, 2816], P(None, 'grp'), may hold values from -0.125 to 0.125
- shared_up: bfloat16 [2048, 2816], P(None, 'grp'), may hold values from -0.125 to 0.125
- shared_down: bfloat16 [2816, 2048], P('grp'), may hold values from -0.109375 to 0.109375
- expert_gate: bfloat16 [128, 2048, 704], P(('grp', 'ep')), may hold values from -0.125 to 0.125
- expert_up: bfloat16 [128, 2048, 704], P(('grp', 'ep')), may hold values from -0.125 to 0.125
- expert_down: bfloat16 [128, 704, 2048], P(('grp', 'ep')), may hold values from -0.15625 to 0.15625
Outputs:
- attended: bfloat16 [16384, 2048], P(('grp', 'ep'))
- moe_update: bfloat16 [16384, 2048], P(('grp', 'ep'))
Inputs may be any that keep to these rules, and one draw needn't show every extreme that they name: `routes`: each row names 6 different experts. The 128 rows of one device name any one expert at most 16 times, and in every draw some device names some expert exactly 16 times. `prompt_lengths`: row g describes group g: its first 4 entries are the lengths of the packed prompts in order, the last one the padding positions at the group's end. Each row sums to 2048, and its largest entry is 1024.
All inputs are finite; a program needn't handle non-finite values.
Results may differ from a plain program's by a relative error of at most 0.015.
The roundings to bfloat16 on the way count: a program that leaves them out, or rounds other values in their place, can miss the bound.
Values may be sent and summed in bfloat16 or wider, within the bound.
A program may use at most 128 MiB of HBM per device.

v0:
```python
import math
import jax
import jax.numpy as jnp
from jax import lax
from jax.sharding import PartitionSpec as P

HDIM = 128
epsilon = 1e-06


def rms_rows(values):
    mean_square = jnp.mean(values * values, axis=-1, keepdims=True)
    return values * lax.rsqrt(mean_square + epsilon)


def segment_ids(length_row, row_total):
    prompt_ends = jnp.cumsum(length_row[:-1])
    positions = jnp.arange(row_total, dtype=jnp.int32)
    segment = jnp.sum((positions[:, None] >= prompt_ends[None, :]).astype(jnp.int32), axis=1)
    return jnp.where(segment >= length_row.shape[0] - 1, -1, segment)


def attend(queries, key_rows, value_rows, segment, block_rows):
    row_total, heads_here, head_dim = queries.shape
    score_scale = 1.0 / math.sqrt(head_dim)
    positions = jnp.arange(row_total, dtype=jnp.int32)

    def one_block(first_row):
        query_block = lax.dynamic_slice_in_dim(queries, first_row, block_rows, 0)
        query_pos = first_row + jnp.arange(block_rows, dtype=jnp.int32)
        query_seg = lax.dynamic_slice_in_dim(segment, first_row, block_rows, 0)
        scores = (
            jnp.einsum("qhd,khd->hqk", query_block, key_rows, preferred_element_type=jnp.float32)
            * score_scale
        )
        allowed = (
            (positions[None, :] <= query_pos[:, None])
            & (segment[None, :] == query_seg[:, None])
            & ((query_seg[:, None] >= 0) | (positions[None, :] == query_pos[:, None]))
        )
        scores = jnp.where(allowed[None], scores, -1e30)
        largest = jnp.max(scores, axis=2, keepdims=True)
        weights = jnp.where(allowed[None], jnp.exp(scores - largest), 0.0)
        totals = jnp.sum(weights, axis=2, keepdims=True)
        attn_probs = (weights / totals).astype(jnp.bfloat16)
        mixed_rows = jnp.einsum(
            "hqk,khd->qhd", attn_probs, value_rows, preferred_element_type=jnp.float32
        )
        return mixed_rows.astype(jnp.bfloat16)

    starts = jnp.arange(row_total // block_rows, dtype=jnp.int32) * block_rows
    blocks = lax.map(one_block, starts)
    return blocks.reshape(row_total, heads_here * head_dim)


def expert_rows(received, gate_half, up_half, down_half):
    width = received.shape[2]
    flattened = received.reshape(-1, width)
    gate_act = jnp.dot(flattened, gate_half, preferred_element_type=jnp.float32)
    up_act = jnp.dot(flattened, up_half, preferred_element_type=jnp.float32)
    hidden = (jax.nn.silu(gate_act) * up_act).astype(jnp.bfloat16)
    partial_value = jnp.dot(hidden, down_half, preferred_element_type=jnp.float32).astype(
        jnp.bfloat16
    )
    return partial_value.reshape(received.shape)


def local(
    hidden_in,
    prompt_lengths,
    routes,
    route_weights,
    w_query,
    w_key,
    w_value,
    w_out,
    shared_gate,
    shared_up,
    shared_down,
    expert_gate,
    expert_up,
    expert_down,
):
    tok_rows, width = hidden_in.shape
    top_count = routes.shape[1]
    grp_count = lax.axis_size("grp")
    ep_count = lax.axis_size("ep")
    device_count = grp_count * ep_count
    expert_count = device_count // 2
    capacity = 8 * tok_rows // expert_count
    group_rows = tok_rows * ep_count
    local_width = w_query.shape[1]
    heads_here = local_width // HDIM
    normed = rms_rows(hidden_in.astype(jnp.float32)).astype(jnp.bfloat16)
    w_joined = jnp.concatenate((w_query, w_key, w_value), axis=1)
    joined = jnp.dot(
        lax.all_gather(normed, "ep", axis=0, tiled=True),
        w_joined,
        preferred_element_type=jnp.float32,
    ).astype(jnp.bfloat16)
    queries = joined[:, :local_width].reshape(group_rows, heads_here, HDIM)
    key_rows = joined[:, local_width : 2 * local_width].reshape(group_rows, heads_here, HDIM)
    value_rows = joined[:, 2 * local_width :].reshape(group_rows, heads_here, HDIM)
    segment = segment_ids(prompt_lengths[0], group_rows)
    heads_local = attend(queries, key_rows, value_rows, segment, min(512, group_rows))
    heads_out = lax.all_to_all(heads_local, "ep", split_axis=0, concat_axis=1, tiled=True)
    residual = hidden_in.astype(jnp.float32) + jnp.dot(
        heads_out, w_out, preferred_element_type=jnp.float32
    )
    normed_moe = rms_rows(residual).astype(jnp.bfloat16)
    gathered = lax.all_gather(normed_moe, "grp", axis=0, tiled=True)
    gate_act = jnp.dot(gathered, shared_gate, preferred_element_type=jnp.float32)
    up_act = jnp.dot(gathered, shared_up, preferred_element_type=jnp.float32)
    hidden = (jax.nn.silu(gate_act) * up_act).astype(jnp.bfloat16)
    shared_out = lax.psum_scatter(
        jnp.dot(hidden, shared_down, preferred_element_type=jnp.float32).astype(jnp.bfloat16),
        "grp",
        scatter_dimension=0,
        tiled=True,
    ).astype(jnp.float32)
    flat_experts = routes.reshape(-1)
    route_total = flat_experts.shape[0]
    onehot = (flat_experts[:, None] == jnp.arange(expert_count, dtype=jnp.int32)[None, :]).astype(
        jnp.int32
    )
    rank_in = jnp.sum((jnp.cumsum(onehot, axis=0) - onehot) * onehot, axis=1)
    slot_index = flat_experts * capacity + rank_in
    token_index = jnp.arange(route_total, dtype=jnp.int32) // top_count
    slot_source = (
        jnp.full((expert_count * capacity,), tok_rows, jnp.int32).at[slot_index].set(token_index)
    )
    padded_rows = jnp.concatenate((normed_moe, jnp.zeros((1, width), jnp.bfloat16)), axis=0)
    outbound = padded_rows[slot_source].reshape(expert_count, 1, capacity, width)
    outbound = jnp.broadcast_to(outbound, (expert_count, 2, capacity, width)).reshape(
        device_count, capacity, width
    )
    gate_half = expert_gate[0]
    up_half = expert_up[0]
    down_half = expert_down[0]
    returned = lax.all_to_all(
        expert_rows(
            lax.all_to_all(outbound, ("grp", "ep"), split_axis=0, concat_axis=0, tiled=True),
            gate_half,
            up_half,
            down_half,
        ),
        ("grp", "ep"),
        split_axis=0,
        concat_axis=0,
        tiled=True,
    )
    by_expert = returned.reshape(expert_count, 2, capacity, width)
    first_half = by_expert[flat_experts, 0, rank_in]
    second_half = by_expert[flat_experts, 1, rank_in]
    expert_sum = first_half.astype(jnp.float32) + second_half.astype(jnp.float32)
    weighted = expert_sum * route_weights.reshape(-1, 1)
    routed = jnp.sum(weighted.reshape(tok_rows, top_count, width), axis=1)
    attended = residual.astype(jnp.bfloat16)
    moe_update = (shared_out + routed).astype(jnp.bfloat16)
    return (attended, moe_update)


def solution(mesh):
    in_specs = (
        P(("grp", "ep"), None),
        P("grp", None),
        P(("grp", "ep"), None),
        P(("grp", "ep"), None),
        P(None, "ep"),
        P(None, "ep"),
        P(None, "ep"),
        P(),
        P(None, "grp"),
        P(None, "grp"),
        P("grp", None),
        P(("grp", "ep"), None, None),
        P(("grp", "ep"), None, None),
        P(("grp", "ep"), None, None),
    )
    out_specs = (P(("grp", "ep"), None), P(("grp", "ep"), None))
    return jax.shard_map(local, mesh=mesh, in_specs=in_specs, out_specs=out_specs, check_vma=False)
```

profile of v0, /device:TPU:37, one launch (start us, length us, event | category | flops | bytes accessed | tf_op | source)
XLA Modules:
  0.0 498.3 jit_solution(996202673333153389)
XLA Ops:
  14.6 68.6 %all-gather.3.cloned.1.call-done = bf16[2048,2048]{1,0:T(8,128)(2,1)} async-done(((bf16[128,2048]{1,0:T(8,128)(2,1)}), bf16[2048,2048]{1,0:T(8,128)(2,1)}) %all-gather.3.cloned.1.call-update) | async-done | bytes 8388624 | tf_op jit(solution)/shard_map/all_gather | solution.py:97
  83.3 8.3 %convolution_convert_fusion.2 = bf16[2048,384]{1,0:T(8,128)(2,1)S(1)} fusion(bf16[2048,2048]{1,0:T(8,128)(2,1)} %all-gather.3.cloned.1.call-done, bf16[2048,128]{1,0:T(8,128)(2,1)} %param.22, bf16[2048,128]{1,0:T(8,128)(2,1)} %param.21, bf16[2048,128]{1,0:T(8,128)(2,1)} %param.20), kind=kOutput, calls=%fused_computation.40 | convolution fusion | flops 3226730496 | bytes 11534336 | tf_op jit(solution)/shard_map/dot_general | solution.py:96
  92.8 53.6 %while.12 = (s32[]{:T(128)}, bf16[4,512,1,128]{3,1,2,0:T(8,128)(2,1)}, s32[4]{0:T(128)S(1)}, s32[2048]{0:T(1024)S(1)}, bf16[2048,1,128]{2,0,1:T(8,128)(2,1)}, /*...) while((s32[]{:T(128)}, ...), condition=%wide.region_6.7_spmd.clone.clone, body=%wide.region_3.6_spmd.clone.clone.sunk | while | flops 570490880 | bytes 16046279 | solution.py:52
  96.3 3.3 fusion.70
  99.6 2.9 fusion.71
  102.5 3.7 fusion.72
  109.7 3.3 fusion.70
  113.0 2.9 fusion.71
  115.9 3.7 fusion.72
  123.1 3.3 fusion.70
  129.3 3.7 fusion.72
  136.5 3.3 fusion.70
  142.7 3.7 fusion.72
  146.4 5.5 %all-to-all-start = ((bf16[16,128,128]{2,1,0:T(8,128)(2,1)}), bf16[16,128,128]{2,1,0:T(8,128)(2,1)}, u32[]{:S(2)}, u32[]{:S(2)}) async-start(bf16[16,128,128]{2,1,0:T(8,128)(2,1)} %bitcast.95), calls=%async_computation | async-start | bytes 1048576 | tf_op jit(solution)/shard_map/all_to_all | solution.py:106
  153.3 3.4 scatter_custom_fusion
  156.7 3.3 all-to-all-done
  162.0 4.9 multiply_reduce_fusion.1
  169.2 6.0 %gather_fusion = bf16[1024,2048]{1,0:T(8,128)(2,1)} fusion(bf16[129,2048]{1,0:T(8,128)(2,1)S(1)} %concatenate.13, s32[1024]{0:T(1024)S(1)} %fusion.42), kind=kCustom, calls=%fused_computation | custom fusion | bytes 8392704 | tf_op jit(solution)/shard_map/gather | solution.py:133
  175.2 6.7 %broadcast_in_dim.43 = bf16[64,2,16,2048]{3,2,1,0:T(8,128)(2,1)} broadcast(bf16[64,16,2048]{2,1,0:T(8,128)(2,1)} %bitcast.92), dimensions={0,2,3} | broadcast | bytes 12582912 | tf_op jit(solution)/shard_map/broadcast_in_dim | solution.py:134
  181.9 10.4 %all-to-all-start.1 = ((bf16[128,16,2048]{2,1,0:T(8,128)(2,1)}), bf16[128,16,2048]{2,1,0:T(8,128)(2,1)}, u32[]{:S(2)}, u32[]{:S(2)}) async-start(bf16[128,16,2048]{2,1,0:T(8,128)(2,1)} %bitcast.91), calls=%async_computation.2 | async-start | bytes 16777216 | tf_op jit(solution)/shard_map/all_to_all | solution.py:142
  193.1 102.8 %all-to-all-done.1 = bf16[128,16,2048]{2,1,0:T(8,128)(2,1)} async-done(((bf16[128,16,2048]{2,1,0:T(8,128)(2,1)}), bf16[128,16,2048]{2,1,0:T(8,128)(2,1)}, u32[]{:S(2)}, u32[]{:S(2)}) %all-to-all-start.1) | async-done | bytes 8388640 | tf_op jit(solution)/shard_map/all_to_all | solution.py:142
  295.9 11.1 %fusion.24 = f32[2048,704]{0,1:T(8,128)} fusion(bf16[2048,2048]{1,0:T(8,128)(2,1)} %bitcast.11, bf16[1,2048,704]{1,2,0:T(8,128)(2,1)} %param.27), kind=kOutput, calls=%fused_computation.37 | convolution fusion | flops 5905580032 | bytes 17039360 | tf_op jit(solution)/shard_map/dot_general | solution.py:59
  307.0 19.1 %convolution_convert_fusion = bf16[2048,2048]{1,0:T(8,128)(2,1)} fusion(f32[2048,704]{0,1:T(8,128)} %fusion.24, bf16[2048,2048]{1,0:T(8,128)(2,1)} %bitcast.11, bf16[1,704,2048]{2,1,0:T(8,128)(2,1)S(1)} %copy-done, bf16[1,2048,704]{1,2,0:T(8,128)(2,1)} %param.28), kind=kOutput, calls=%fused_computation.31 | convolution fusion | flops 11824005120 | bytes 28311552 | tf_op jit(solution)/shard_map/dot_general | solution.py:62
  326.0 6.2 %all-to-all-start.2 = ((bf16[128,16,2048]{2,1,0:T(8,128)(2,1)}), bf16[128,16,2048]{2,1,0:T(8,128)(2,1)}, u32[]{:S(2)}, u32[]{:S(2)}) async-start(bf16[128,16,2048]{2,1,0:T(8,128)(2,1)} %bitcast.93), calls=%async_computation.3 | async-start | bytes 16777216 | tf_op jit(solution)/shard_map/all_to_all | solution.py:140
  332.5 5.4 %fusion.54 = f32[1024,352]{0,1:T(8,128)} fusion(bf16[1024,2048]{1,0:T(8,128)(2,1)} %all-gather.5.cloned.1.call-done, bf16[2048,352]{0,1:T(8,128)(2,1)} %param.24), kind=kOutput, calls=%fused_computation.100 | convolution fusion | flops 1476395008 | bytes 7077888 | tf_op jit(solution)/shard_map/dot_general | solution.py:112
  337.9 9.4 %convolution_convert_fusion.1 = bf16[1024,2048]{1,0:T(8,128)(2,1)} fusion(bf16[352,2048]{1,0:T(8,128)(2,1)} %param.26, bf16[1024,2048]{1,0:T(8,128)(2,1)} %all-gather.5.cloned.1.call-done, bf16[2048,352]{0,1:T(8,128)(2,1)} %param.25, f32[1024,352]{0,1:T(8,128)} %fusion.54), kind=kOutput, calls=%fused_computation.34 | convolution fusion | flops 2957049856 | bytes 12713984 | tf_op jit(solution)/shard_map/dot_general | solution.py:116
  348.1 87.8 %all-to-all-done.2 = bf16[128,16,2048]{2,1,0:T(8,128)(2,1)} async-done(((bf16[128,16,2048]{2,1,0:T(8,128)(2,1)}), bf16[128,16,2048]{2,1,0:T(8,128)(2,1)}, u32[]{:S(2)}, u32[]{:S(2)}) %all-to-all-start.2) | async-done | bytes 8388640 | tf_op jit(solution)/shard_map/all_to_all | solution.py:140
  435.8 15.4 %gather_fusion.2 = bf16[768,2048]{1,0:T(8,128)(2,1)} fusion(bf16[64,2,16,2048]{3,2,1,0:T(8,128)(2,1)} %bitcast.16, s32[768]{0:T(1024)S(1)} %get-tuple-element.92), kind=kCustom, calls=%fused_computation.2 | custom fusion | bytes 6300672 | tf_op jit(solution)/shard_map/gather | solution.py:154
  451.3 15.5 %gather_fusion.1 = bf16[768,2048]{1,0:T(8,128)(2,1)} fusion(bf16[64,2,16,2048]{3,2,1,0:T(8,128)(2,1)} %bitcast.16, s32[768]{0:T(1024)S(1)} %get-tuple-element.91), kind=kCustom, calls=%fused_computation.1 | custom fusion | bytes 6300672 | tf_op jit(solution)/shard_map/gather | solution.py:153
  466.8 6.9 %convert_add_fusion = f32[768,2048]{1,0:T(8,128)} fusion(bf16[768,2048]{1,0:T(8,128)(2,1)} %gather_fusion.2, bf16[768,2048]{1,0:T(8,128)(2,1)} %gather_fusion.1), kind=kLoop, calls=%fused_computation.32 | loop fusion | flops 4718592 | bytes 12582912 | tf_op jit(solution)/shard_map/add | solution.py:155
  473.7 7.8 %add.123 = f32[128,6,2048]{2,1,0:T(8,128)} reshape(f32[768,2048]{1,0:T(8,128)} %convert_add_fusion) | data formatting | bytes 12582912 | tf_op jit(solution)/shard_map/add | solution.py:155
  481.5 7.6 %multiply_reduce_fusion = f32[128,2048]{1,0:T(8,128)} fusion(f32[128,6,2048]{2,1,0:T(8,128)} %add.123, f32[128,6]{1,0:T(8,128)S(1)} %copy.36), kind=kLoop, calls=%fused_computation.30 | loop fusion | flops 2883584 | bytes 7343104 | tf_op jit(solution)/shard_map/reduce_sum | solution.py:157
  (66 shorter events, 29.9 us)
Async XLA Ops:
  7.2 299.8 %copy-start = (bf16[1,704,2048]{2,1,0:T(8,128)(2,1)S(1)}, bf16[1,704,2048]{2,1,0:T(8,128)(2,1)}, u32[]{:S(2)}) copy-start(bf16[1,704,2048]{2,1,0:T(8,128)(2,1)} %param.29) | copy-start | bytes 8650756
  7.2 76.1 %all-gather.3.cloned.1.call-start = ((), (), s32[]{:S(2)}) async-start(), calls=%async_computation.4 | async-start | bytes 8912896 | tf_op jit(solution)/shard_map/all_gather | solution.py:97
  14.2 77.3 %copy-start.2 = (s32[64,6,128]{2,0,1:T(8,128)}, s32[64,6,128]{2,0,1:T(8,128)S(1)}, u32[]{:S(2)}) copy-start(s32[64,6,128]{2,0,1:T(8,128)S(1)} %reduce-window.19) | copy-start | bytes 589828
  92.8 69.3 %copy-start.1 = (bf16[128,2048]{1,0:T(8,128)(2,1)S(1)}, bf16[128,2048]{1,0:T(8,128)(2,1)}, u32[]{:S(2)}) copy-start(bf16[128,2048]{1,0:T(8,128)(2,1)} %param.16) | copy-start | bytes 1572868
  99.6 2.9 copy-start.3
  113.0 2.9 copy-start.3
  126.4 2.9 copy-start.3
  139.8 2.9 copy-start.3
  146.4 13.6 %all-to-all-start = ((bf16[16,128,128]{2,1,0:T(8,128)(2,1)}), bf16[16,128,128]{2,1,0:T(8,128)(2,1)}, u32[]{:S(2)}, u32[]{:S(2)}) async-start(bf16[16,128,128]{2,1,0:T(8,128)(2,1)} %bitcast.95), calls=%async_computation | async-start | bytes 1048576 | tf_op jit(solution)/shard_map/all_to_all | solution.py:106
  181.9 113.9 %all-to-all-start.1 = ((bf16[128,16,2048]{2,1,0:T(8,128)(2,1)}), bf16[128,16,2048]{2,1,0:T(8,128)(2,1)}, u32[]{:S(2)}, u32[]{:S(2)}) async-start(bf16[128,16,2048]{2,1,0:T(8,128)(2,1)} %bitcast.91), calls=%async_computation.2 | async-start | bytes 16777216 | tf_op jit(solution)/shard_map/all_to_all | solution.py:142
  192.3 140.2 %all-gather.5.cloned.1.call-start = ((), (), s32[]{:S(2)}) async-start(), calls=%async_computation.5 | async-start | bytes 4718592 | tf_op jit(solution)/shard_map/all_gather | solution.py:111
  326.0 109.8 %all-to-all-start.2 = ((bf16[128,16,2048]{2,1,0:T(8,128)(2,1)}), bf16[128,16,2048]{2,1,0:T(8,128)(2,1)}, u32[]{:S(2)}, u32[]{:S(2)}) async-start(bf16[128,16,2048]{2,1,0:T(8,128)(2,1)} %bitcast.93), calls=%async_computation.3 | async-start | bytes 16777216 | tf_op jit(solution)/shard_map/all_to_all | solution.py:140
  332.2 156.9 %reduce-scatter.2.cloned.1.call-start = ((), (), s32[]{:S(2)}) async-start(), calls=%async_computation.6 | async-start | bytes 4718592 | tf_op jit(solution)/shard_map/reduce_scatter | solution.py:115
  347.3 0.7 copy-start.4
Sparse Core Ops, SparseCore 0:
  10.8 72.4 all-gather.2
  195.4 107.2 all-gather.4
  347.4 100.0 reduce-scatter.1
where the time goes:
time: 507 us; the launch traced here: 498 us
  waiting for transfers between devices  263 us (52%)
  matrix products  86.1 us (17%)
  local copies, waits for them, and re-layouts  64.9 us (13%)
  other arithmetic  39.1 us (8%)
  starting transfers between devices  22.4 us (4%)
  between operations  14.3 us (3%)
  loops' own time  8.41 us (2%)
    all_to_all x1, waiting for transfers between devices, local(): lax.all_to_all(outbound, ('grp', 'ep'), split_axis=0, concat_axis=0, tile...  103 us
    all_to_all x1, waiting for transfers between devices, local(): lax.all_to_all(expert_rows(lax.all_to_all(outbound, ('grp', 'ep'), split_...  87.8 us
    all_gather x1, waiting for transfers between devices, local(): lax.all_gather(normed, 'ep', axis=0, tiled=True)  68.6 us
    dot_general x1, matrix products, expert_rows(): jnp.dot(hidden, down_half, preferred_element_type=jnp.float32)  19.1 us
    gather x1, local copies, waits for them, and re-layouts, local(): first_half = by_expert[flat_experts, 0, rank_in]  15.5 us
    gather x1, local copies, waits for them, and re-layouts, local(): second_half = by_expert[flat_experts, 1, rank_in]  15.4 us
    dot_general x4, matrix products, one_block(): jnp.einsum('hqk,khd->qhd', attn_probs, value_rows, preferred_element_type...  14.8 us
    dot_general x4, matrix products, one_block(): jnp.einsum('qhd,khd->hqk', query_block, key_rows, preferred_element_type=...  13.2 us
  transfers between devices with their start and end apart: 6, of which 4 were waited for; matrix products, arithmetic and copies ran while one was open for 21% of the time, Pallas kernels for 0%

commit v1 on v0

--- a/solution.py
+++ b/solution.py
@@ -93,11 +93,21 @@
     heads_here = local_width // HDIM
     normed = rms_rows(hidden_in.astype(jnp.float32)).astype(jnp.bfloat16)
     w_joined = jnp.concatenate((w_query, w_key, w_value), axis=1)
-    joined = jnp.dot(
-        lax.all_gather(normed, "ep", axis=0, tiled=True),
-        w_joined,
-        preferred_element_type=jnp.float32,
-    ).astype(jnp.bfloat16)
+
+    def use_region(array_in):
+        return jnp.concatenate(
+            jax.lax.all_to_all(
+                jnp.stack([array_in for _ in range(jax.lax.axis_size("ep"))], 0),
+                "ep",
+                split_axis=0,
+                concat_axis=0,
+            ),
+            0,
+        )
+
+    joined = jnp.dot(use_region(normed), w_joined, preferred_element_type=jnp.float32).astype(
+        jnp.bfloat16
+    )
     queries = joined[:, :local_width].reshape(group_rows, heads_here, HDIM)
     key_rows = joined[:, local_width : 2 * local_width].reshape(group_rows, heads_here, HDIM)
     value_rows = joined[:, 2 * local_width :].reshape(group_rows, heads_here, HDIM)

time: 507 us -> 597 us (1.18)
  waiting for transfers between devices: 263 us -> 320 us
  starting transfers between devices: 22.4 us -> 52 us
    all_to_all x0 -> x1, waiting for transfers between devices: none -> 127 us  [use_region(): jax.lax.all_to_all(jnp.stack([array_in for _ in range(jax.lax.axis_size('...]
    all_gather x1 -> x0, waiting for transfers between devices: 68.6 us -> none  [local(): lax.all_gather(normed, 'ep', axis=0, tiled=True)]
    all_to_all x1, starting transfers between devices: 5.48 us -> 25.5 us  [local(): lax.all_to_all(heads_local, 'ep', split_axis=0, concat_axis=1, tiled=True)]
    all_to_all x0 -> x1, starting transfers between devices: none -> 7.02 us  [use_region(): jax.lax.all_to_all(jnp.stack([array_in for _ in range(jax.lax.axis_size('...]
  transfers between devices with their start and end apart: 6 -> 6, of which waited for: 4 -> 4; matrix products, arithmetic and copies ran while one was open for 21% -> 18% of each run, Pallas kernels for 0% -> 0%
where the time goes in v1:
time: 597 us; the launch traced here: 587 us
  waiting for transfers between devices  320 us (54%)
  matrix products  86.1 us (14%)
  local copies, waits for them, and re-layouts  67.8 us (11%)
  starting transfers between devices  52 us (9%)
  other arithmetic  38.3 us (6%)
  between operations  14.6 us (2%)
  loops' own time  8.41 us (1%)
    all_to_all x1, waiting for transfers between devices, use_region(): jax.lax.all_to_all(jnp.stack([array_in for _ in range(jax.lax.axis_size('...  127 us
    all_to_all x1, waiting for transfers between devices, local(): lax.all_to_all(outbound, ('grp', 'ep'), split_axis=0, concat_axis=0, tile...  103 us
    all_to_all x1, waiting for transfers between devices, local(): lax.all_to_all(expert_rows(lax.all_to_all(outbound, ('grp', 'ep'), split_...  87.8 us
    all_to_all x1, starting transfers between devices, local(): lax.all_to_all(heads_local, 'ep', split_axis=0, concat_axis=1, tiled=True)  25.5 us
    dot_general x1, matrix products, expert_rows(): jnp.dot(hidden, down_half, preferred_element_type=jnp.float32)  19.1 us
    gather x1, local copies, waits for them, and re-layouts, local(): first_half = by_expert[flat_experts, 0, rank_in]  15.5 us
    gather x1, local copies, waits for them, and re-layouts, local(): second_half = by_expert[flat_experts, 1, rank_in]  15.4 us
    dot_general x4, matrix products, one_block(): jnp.einsum('hqk,khd->qhd', attn_probs, value_rows, preferred_element_type...  14.8 us
  transfers between devices with their start and end apart: 6, of which 4 were waited for; matrix products, arithmetic and copies ran while one was open for 18% of the time, Pallas kernels for 0%

profile of v1, /device:TPU:37, one launch (start us, length us, event | category | flops | bytes accessed | tf_op | source)
XLA Modules:
  0.0 587.3 jit_solution(4703839225427605317)
XLA Ops:
  9.8 4.3 stack.2
  14.1 7.0 %all-to-all-start = ((bf16[16,128,2048]{2,1,0:T(8,128)(2,1)}), bf16[16,128,2048]{2,1,0:T(8,128)(2,1)}, u32[]{:S(2)}, u32[]{:S(2)}) async-start(bf16[16,128,2048]{2,1,0:T(8,128)(2,1)} %stack.2), calls=%async_computation | async-start | bytes 16777216 | tf_op jit(solution)/shard_map/all_to_all | solution.py:99
  23.8 126.8 %all-to-all-done = bf16[16,128,2048]{2,1,0:T(8,128)(2,1)} async-done(((bf16[16,128,2048]{2,1,0:T(8,128)(2,1)}), bf16[16,128,2048]{2,1,0:T(8,128)(2,1)}, u32[]{:S(2)}, u32[]{:S(2)}) %all-to-all-start) | async-done | bytes 8388640 | tf_op jit(solution)/shard_map/all_to_all | solution.py:99
  150.6 8.3 %convolution_convert_fusion.2 = bf16[2048,384]{1,0:T(8,128)(2,1)S(1)} fusion(bf16[2048,2048]{1,0:T(8,128)(2,1)} %bitcast.2, bf16[2048,128]{1,0:T(8,128)(2,1)} %param.22, bf16[2048,128]{1,0:T(8,128)(2,1)} %param.21, bf16[2048,128]{1,0:T(8,128)(2,1)} %param.20), kind=kOutput, calls=%fused_computation.40 | convolution fusion | flops 3226730496 | bytes 11534336 | tf_op jit(solution)/shard_map/dot_general | solution.py:108
  160.1 53.6 %while.12 = (s32[]{:T(128)}, bf16[4,512,1,128]{3,1,2,0:T(8,128)(2,1)}, s32[4]{0:T(128)S(1)}, s32[2048]{0:T(1024)S(1)}, bf16[2048,1,128]{2,0,1:T(8,128)(2,1)}, /*...) while((s32[]{:T(128)}, ...), condition=%wide.region_6.7_spmd.clone.clone, body=%wide.region_3.6_spmd.clone.clone.sunk | while | flops 570490880 | bytes 16046279 | solution.py:52
  163.6 3.3 fusion.70
  166.9 2.9 fusion.71
  169.8 3.7 fusion.72
  177.0 3.3 fusion.70
  183.2 3.7 fusion.72
  190.5 3.3 fusion.70
  196.6 3.7 fusion.72
  203.9 3.3 fusion.70
  210.0 3.7 fusion.72
  213.7 25.5 %all-to-all-start.1 = ((bf16[16,128,128]{2,1,0:T(8,128)(2,1)}), bf16[16,128,128]{2,1,0:T(8,128)(2,1)}, u32[]{:S(2)}, u32[]{:S(2)}) async-start(bf16[16,128,128]{2,1,0:T(8,128)(2,1)} %bitcast.96), calls=%async_computation.1 | async-start | bytes 1048576 | tf_op jit(solution)/shard_map/all_to_all | solution.py:116
  240.7 3.4 scatter_custom_fusion
  248.1 4.9 multiply_reduce_fusion.1
  255.2 6.0 %gather_fusion = bf16[1024,2048]{1,0:T(8,128)(2,1)} fusion(bf16[129,2048]{1,0:T(8,128)(2,1)S(1)} %concatenate.13, s32[1024]{0:T(1024)S(1)} %fusion.42), kind=kCustom, calls=%fused_computation | custom fusion | bytes 8392704 | tf_op jit(solution)/shard_map/gather | solution.py:143
  261.3 6.7 %broadcast_in_dim.43 = bf16[64,2,16,2048]{3,2,1,0:T(8,128)(2,1)} broadcast(bf16[64,16,2048]{2,1,0:T(8,128)(2,1)} %bitcast.93), dimensions={0,2,3} | broadcast | bytes 12582912 | tf_op jit(solution)/shard_map/broadcast_in_dim | solution.py:144
  268.0 13.0 %all-to-all-start.2 = ((bf16[128,16,2048]{2,1,0:T(8,128)(2,1)}), bf16[128,16,2048]{2,1,0:T(8,128)(2,1)}, u32[]{:S(2)}, u32[]{:S(2)}) async-start(bf16[128,16,2048]{2,1,0:T(8,128)(2,1)} %bitcast.92), calls=%async_computation.3 | async-start | bytes 16777216 | tf_op jit(solution)/shard_map/all_to_all | solution.py:152
  281.8 102.8 %all-to-all-done.2 = bf16[128,16,2048]{2,1,0:T(8,128)(2,1)} async-done(((bf16[128,16,2048]{2,1,0:T(8,128)(2,1)}), bf16[128,16,2048]{2,1,0:T(8,128)(2,1)}, u32[]{:S(2)}, u32[]{:S(2)}) %all-to-all-start.2) | async-done | bytes 8388640 | tf_op jit(solution)/shard_map/all_to_all | solution.py:152
  384.6 11.1 %fusion.24 = f32[2048,704]{0,1:T(8,128)} fusion(bf16[2048,2048]{1,0:T(8,128)(2,1)} %bitcast.12, bf16[1,2048,704]{1,2,0:T(8,128)(2,1)} %param.27), kind=kOutput, calls=%fused_computation.37 | convolution fusion | flops 5905580032 | bytes 17039360 | tf_op jit(solution)/shard_map/dot_general | solution.py:59
  395.7 19.1 %convolution_convert_fusion = bf16[2048,2048]{1,0:T(8,128)(2,1)} fusion(f32[2048,704]{0,1:T(8,128)} %fusion.24, bf16[2048,2048]{1,0:T(8,128)(2,1)} %bitcast.12, bf16[1,704,2048]{2,1,0:T(8,128)(2,1)S(1)} %copy-done, bf16[1,2048,704]{1,2,0:T(8,128)(2,1)} %param.28), kind=kOutput, calls=%fused_computation.31 | convolution fusion | flops 11824005120 | bytes 28311552 | tf_op jit(solution)/shard_map/dot_general | solution.py:62
  414.7 6.2 %all-to-all-start.3 = ((bf16[128,16,2048]{2,1,0:T(8,128)(2,1)}), bf16[128,16,2048]{2,1,0:T(8,128)(2,1)}, u32[]{:S(2)}, u32[]{:S(2)}) async-start(bf16[128,16,2048]{2,1,0:T(8,128)(2,1)} %bitcast.94), calls=%async_computation.4 | async-start | bytes 16777216 | tf_op jit(solution)/shard_map/all_to_all | solution.py:150
  421.2 5.4 fusion.54
  426.6 9.4 %convolution_convert_fusion.1 = bf16[1024,2048]{1,0:T(8,128)(2,1)} fusion(bf16[352,2048]{1,0:T(8,128)(2,1)} %param.26, bf16[1024,2048]{1,0:T(8,128)(2,1)} %all-gather.2.cloned.1.call-done, bf16[2048,352]{0,1:T(8,128)(2,1)} %param.25, f32[1024,352]{0,1:T(8,128)} %fusion.54), kind=kOutput, calls=%fused_computation.34 | convolution fusion | flops 2957049856 | bytes 12713984 | tf_op jit(solution)/shard_map/dot_general | solution.py:126
  436.8 87.8 %all-to-all-done.3 = bf16[128,16,2048]{2,1,0:T(8,128)(2,1)} async-done(((bf16[128,16,2048]{2,1,0:T(8,128)(2,1)}), bf16[128,16,2048]{2,1,0:T(8,128)(2,1)}, u32[]{:S(2)}, u32[]{:S(2)}) %all-to-all-start.3) | async-done | bytes 8388640 | tf_op jit(solution)/shard_map/all_to_all | solution.py:150
  524.5 15.4 %gather_fusion.2 = bf16[768,2048]{1,0:T(8,128)(2,1)} fusion(bf16[64,2,16,2048]{3,2,1,0:T(8,128)(2,1)} %bitcast.17, s32[768]{0:T(1024)S(1)} %get-tuple-element.92), kind=kCustom, calls=%fused_computation.2 | custom fusion | bytes 6300672 | tf_op jit(solution)/shard_map/gather | solution.py:164
  540.0 15.5 %gather_fusion.1 = bf16[768,2048]{1,0:T(8,128)(2,1)} fusion(bf16[64,2,16,2048]{3,2,1,0:T(8,128)(2,1)} %bitcast.17, s32[768]{0:T(1024)S(1)} %get-tuple-element.91), kind=kCustom, calls=%fused_computation.1 | custom fusion | bytes 6300672 | tf_op jit(solution)/shard_map/gather | solution.py:163
  555.5 6.9 %convert_add_fusion = f32[768,2048]{1,0:T(8,128)} fusion(bf16[768,2048]{1,0:T(8,128)(2,1)} %gather_fusion.2, bf16[768,2048]{1,0:T(8,128)(2,1)} %gather_fusion.1), kind=kLoop, calls=%fused_computation.32 | loop fusion | flops 4718592 | bytes 12582912 | tf_op jit(solution)/shard_map/add | solution.py:165
  562.4 7.8 %add.123 = f32[128,6,2048]{2,1,0:T(8,128)} reshape(f32[768,2048]{1,0:T(8,128)} %convert_add_fusion) | data formatting | bytes 12582912 | tf_op jit(solution)/shard_map/add | solution.py:165
  570.2 7.6 %multiply_reduce_fusion = f32[128,2048]{1,0:T(8,128)} fusion(f32[128,6,2048]{2,1,0:T(8,128)} %add.123, f32[128,6]{1,0:T(8,128)S(1)} %copy.36), kind=kLoop, calls=%fused_computation.30 | loop fusion | flops 2883584 | bytes 7343104 | tf_op jit(solution)/shard_map/reduce_sum | solution.py:167
  (70 shorter events, 32.5 us)
Async XLA Ops:
  7.2 388.5 %copy-start = (bf16[1,704,2048]{2,1,0:T(8,128)(2,1)S(1)}, bf16[1,704,2048]{2,1,0:T(8,128)(2,1)}, u32[]{:S(2)}) copy-start(bf16[1,704,2048]{2,1,0:T(8,128)(2,1)} %param.29) | copy-start | bytes 8650756
  14.1 7.0 %copy-start.6 = (s32[1,5]{1,0:T(1,128)S(1)}, s32[1,5]{1,0:T(1,128)}, u32[]{:S(2)}) copy-start(s32[1,5]{1,0:T(1,128)} %param.17) | copy-start | bytes 64
  14.1 7.2 %copy-start.4 = (s32[128,6]{0,1:T(8,128)S(1)}, s32[128,6]{0,1:T(8,128)}, u32[]{:S(2)}) copy-start(s32[128,6]{0,1:T(8,128)} %param.18) | copy-start | bytes 9220
  14.1 136.5 %all-to-all-start = ((bf16[16,128,2048]{2,1,0:T(8,128)(2,1)}), bf16[16,128,2048]{2,1,0:T(8,128)(2,1)}, u32[]{:S(2)}, u32[]{:S(2)}) async-start(bf16[16,128,2048]{2,1,0:T(8,128)(2,1)} %stack.2), calls=%async_computation | async-start | bytes 16777216 | tf_op jit(solution)/shard_map/all_to_all | solution.py:99
  23.4 135.5 %copy-start.2 = (s32[64,6,128]{2,0,1:T(8,128)}, s32[64,6,128]{2,0,1:T(8,128)S(1)}, u32[]{:S(2)}) copy-start(s32[64,6,128]{2,0,1:T(8,128)S(1)} %reduce-window.19) | copy-start | bytes 589828
  160.1 88.0 %copy-start.1 = (bf16[128,2048]{1,0:T(8,128)(2,1)S(1)}, bf16[128,2048]{1,0:T(8,128)(2,1)}, u32[]{:S(2)}) copy-start(bf16[128,2048]{1,0:T(8,128)(2,1)} %param.16) | copy-start | bytes 1572868
  166.9 2.9 copy-start.3
  180.3 2.9 copy-start.3
  193.8 2.9 copy-start.3
  207.2 2.9 copy-start.3
  213.7 32.3 %all-to-all-start.1 = ((bf16[16,128,128]{2,1,0:T(8,128)(2,1)}), bf16[16,128,128]{2,1,0:T(8,128)(2,1)}, u32[]{:S(2)}, u32[]{:S(2)}) async-start(bf16[16,128,128]{2,1,0:T(8,128)(2,1)} %bitcast.96), calls=%async_computation.1 | async-start | bytes 1048576 | tf_op jit(solution)/shard_map/all_to_all | solution.py:116
  268.0 116.6 %all-to-all-start.2 = ((bf16[128,16,2048]{2,1,0:T(8,128)(2,1)}), bf16[128,16,2048]{2,1,0:T(8,128)(2,1)}, u32[]{:S(2)}, u32[]{:S(2)}) async-start(bf16[128,16,2048]{2,1,0:T(8,128)(2,1)} %bitcast.92), calls=%async_computation.3 | async-start | bytes 16777216 | tf_op jit(solution)/shard_map/all_to_all | solution.py:152
  281.0 140.2 %all-gather.2.cloned.1.call-start = ((), (), s32[]{:S(2)}) async-start(), calls=%async_computation.5 | async-start | bytes 4718592 | tf_op jit(solution)/shard_map/all_gather | solution.py:121
  414.7 109.8 %all-to-all-start.3 = ((bf16[128,16,2048]{2,1,0:T(8,128)(2,1)}), bf16[128,16,2048]{2,1,0:T(8,128)(2,1)}, u32[]{:S(2)}, u32[]{:S(2)}) async-start(bf16[128,16,2048]{2,1,0:T(8,128)(2,1)} %bitcast.94), calls=%async_computation.4 | async-start | bytes 16777216 | tf_op jit(solution)/shard_map/all_to_all | solution.py:150
  420.9 156.9 %reduce-scatter.2.cloned.1.call-start = ((), (), s32[]{:S(2)}) async-start(), calls=%async_computation.6 | async-start | bytes 4718592 | tf_op jit(solution)/shard_map/reduce_scatter | solution.py:125
  436.0 0.7 copy-start.5
Sparse Core Ops, SparseCore 0:
  284.1 107.2 all-gather.1
  436.1 100.0 reduce-scatter.1
